TPU v7x, 32 devices: a whole 2x2x4 slice. The times are simulated.
32 devices in a mesh: dp: 4 (over z), adapter: 8 (over y, x, core).
Axes of the slice: x: 2, y: 2, z: 4, core: 2. Of those that a mesh axis runs over, the one named last changes fastest.
Arguments:
- states: bfloat16 [2, 1024, 8192], P(None, ('dp', 'adapter')), may hold values from -6 to 6
- request_slot_index: int32 [2, 1024, 1], P(None, ('dp', 'adapter')), may hold values from 0 to 7; in each aligned block of 32 rows (0 to 31, 32 to 63, ..., all dimensions but the last counted through in order) at most 8 rows name the same one
- down_weights: bfloat16 [32, 64, 8192], P(('dp', 'adapter')), may hold values from -0.0625 to 0.0625
- up_weights: bfloat16 [32, 64, 8192], P(('dp', 'adapter')), may hold values from -0.75 to 0.75
- active_adapter_owner: int32 [2, 8], replicated, may hold values from 0 to 3
Outputs:
- delta: bfloat16 [2, 1024, 8192], P(None, ('dp', 'adapter'))
Inputs may be any that keep to these rules, and one draw needn't show every extreme that they name: `request_slot_index`: within the rows of one device at one step (aligned blocks of 32 rows), no column is named by more than 8 rows, a bound that some block reaches.
All inputs are finite; a program needn't handle non-finite values.
Results may differ from a plain program's by a relative error of at most 0.0049.
Values may be sent and summed in bfloat16 or wider, within the bound.
A program may use at most 64 MiB of HBM per device.

v0:
```python
import jax
import jax.numpy as jnp
from jax import lax
from jax.sharding import PartitionSpec as P


def from_root(array, axis, root):
    mine = lax.axis_index(axis) == root
    return lax.psum(jnp.where(mine, array, jnp.zeros_like(array)), axis)


def slot_matrix(column_ids, columns, capacity):
    hits = (column_ids[:, None] == jnp.arange(columns, dtype=jnp.int32)[None, :]).astype(jnp.int32)
    slot_rank = jnp.sum(jnp.cumsum(hits, axis=0) * hits, axis=1) - 1
    target = column_ids * capacity + slot_rank
    return (target[:, None] == jnp.arange(columns * capacity, dtype=jnp.int32)[None, :]).astype(
        jnp.bfloat16
    )


def project(arrived, stack_down, stack_up):
    low_rank = jnp.einsum(
        "scnd,srd->scnr", arrived, stack_down, preferred_element_type=jnp.float32
    ).astype(jnp.bfloat16)
    return jnp.einsum(
        "scnr,srd->scnd", low_rank, stack_up, preferred_element_type=jnp.float32
    ).astype(jnp.bfloat16)


def serve_one(arrived, stack_down, stack_up):
    result = project(arrived, stack_down, stack_up)
    return lax.all_to_all(result, "adapter", split_axis=1, concat_axis=1, tiled=True)


def body(states, request_slot_index, down_weights, up_weights, active_adapter_owner):
    step_count = states.shape[0]
    rows_dev = states.shape[1]
    model_width = states.shape[2]
    columns = lax.axis_size("adapter")
    column_index = lax.axis_index("adapter")
    capacity = max(2, 2 * rows_dev // columns)
    slot_count = columns * capacity
    downs = []
    uppers = []
    for step_index in range(step_count):
        owner_leader = active_adapter_owner[step_index, column_index]
        got_down, got_up = (
            from_root(down_weights[0], "dp", owner_leader),
            from_root(up_weights[0], "dp", owner_leader),
        )
        downs.append(got_down)
        uppers.append(got_up)
    stack_down = jnp.stack(downs)
    stack_up = jnp.stack(uppers)
    placements = []
    outgoing_list = []
    for step_index in range(step_count):
        placement = slot_matrix(request_slot_index[step_index, :, 0], columns, capacity)
        placements.append(placement)
        packed = lax.dot_general(
            placement,
            states[step_index],
            (((0,), (0,)), ((), ())),
            preferred_element_type=jnp.float32,
        )
        outgoing_list.append(packed.astype(jnp.bfloat16).reshape(columns, capacity, model_width))
    outgoing = jnp.stack(outgoing_list)
    returned_list = []
    for step_index in range(step_count):
        returned_list.append(
            serve_one(
                lax.all_to_all(
                    outgoing[step_index : step_index + 1],
                    "adapter",
                    split_axis=1,
                    concat_axis=1,
                    tiled=True,
                ),
                stack_down=stack_down[step_index : step_index + 1],
                stack_up=stack_up[step_index : step_index + 1],
            )
        )
    returned_rows = jnp.concatenate(returned_list, axis=0)
    delta_list = []
    for step_index in range(step_count):
        flat_rows = returned_rows[step_index].reshape(slot_count, model_width)
        delta_list.append(
            jnp.dot(placements[step_index], flat_rows, preferred_element_type=jnp.float32).astype(
                jnp.bfloat16
            )
        )
    return jnp.stack(delta_list)


def solution(mesh):
    return jax.shard_map(
        body,
        mesh=mesh,
        in_specs=(
            P(None, ("dp", "adapter"), None),
            P(None, ("dp", "adapter"), None),
            P(("dp", "adapter"), None, None),
            P(("dp", "adapter"), None, None),
            P(),
        ),
        out_specs=P(None, ("dp", "adapter"), None),
        check_vma=False,
    )
```

profile of v0, /device:TPU:0, one launch (start us, length us, event | category | flops | bytes accessed | tf_op | source)
XLA Modules:
  0.0 222.1 jit_solution(10519682711103507936)
XLA Ops:
  6.5 1.4 constant_dynamic-slice_fusion.1
  9.3 3.7 %select_bitcast_fusion.2 = (bf16[64,8192]{1,0:T(8,128)(2,1)}, bf16[64,8192]{1,0:T(8,128)(2,1)}, bf16[64,8192]{1,0:T(8,128)(2,1)}, bf16[64,8192]{1,0:T(8,128)(2,1)}) fusion(bf16[1,64,8192]{2,1,0:T(8,128)(2,1)} %param.8, pred[]{:T(512)S(6)} %eq.66, pred[]{:T(512)S(6)} %eq.73, bf16[1,64,8192]{2,1,0:T(8,128)(2,1)} %param.7), kind=kLoop, calls=%fused_computation.25 | loop fusion | flops 2097152 | bytes 6291458 | tf_op jit(solution)/shard_map/jit(_where)/select_n | solution.py:9
  13.0 0.7 copy-done.2
  13.6 0.1 fusion.23
  13.7 0.1 reduce_window_sum.17
  13.8 0.1 fusion.22
  13.8 0.1 reduce_window_sum.18
  13.9 0.2 select_reduce_fusion
  14.1 0.1 copy-done
  14.2 1.6 fusion
  15.8 5.2 %all-to-all-start = ((bf16[1,8,8,8192]{3,2,0,1:T(8,128)(2,1)}), bf16[1,8,8,8192]{3,2,0,1:T(8,128)(2,1)S(1)}, u32[]{:S(2)}, u32[]{:S(2)}) async-start(bf16[1,8,8,8192]{3,2,0,1:T(8,128)(2,1)} %fusion), calls=%async_computation | async-start | bytes 2097152 | tf_op jit(solution)/shard_map/all_to_all | solution.py:72
  21.0 1.6 fusion.2
  22.5 13.8 %all-to-all-done = bf16[1,8,8,8192]{3,2,0,1:T(8,128)(2,1)S(1)} async-done(((bf16[1,8,8,8192]{3,2,0,1:T(8,128)(2,1)}), bf16[1,8,8,8192]{3,2,0,1:T(8,128)(2,1)S(1)}, u32[]{:S(2)}, u32[]{:S(2)}) %all-to-all-start) | async-done | bytes 1048608 | tf_op jit(solution)/shard_map/all_to_all | solution.py:72
  36.4 3.6 %all-to-all-start.2 = ((bf16[1,8,8,8192]{3,2,0,1:T(8,128)(2,1)}), bf16[1,8,8,8192]{3,2,0,1:T(8,128)(2,1)S(1)}, u32[]{:S(2)}, u32[]{:S(2)}) async-start(bf16[1,8,8,8192]{3,2,0,1:T(8,128)(2,1)} %fusion.2), calls=%async_computation.2 | async-start | bytes 2097152 | tf_op jit(solution)/shard_map/all_to_all | solution.py:72
  39.9 131.9 %all-reduce.3.cloned.1.call-done = (bf16[64,8192]{1,0:T(8,128)(2,1)}, bf16[64,8192]{1,0:T(8,128)(2,1)}, bf16[64,8192]{1,0:T(8,128)(2,1)}, bf16[64,8192]{1,0:T(8,128)(2,1)}) async-done(((bf16[64,8192]{1,0:T(8,128)(2,1)}, bf16[64,8192]{1,0:T(8,128)(2,1)}, bf16[64,8192]{1,0:T(8,128)(2,1)}, bf16[64,8192]{1,0:T(8,128)(2,1)}), (bf16[64,8192]{1,0:T(8,128)(2,1)}, bf16[64,8192]{1,0:T(8,128)(2,1)}, ...) | async-done | bytes 4194320 | tf_op jit(solution)/shard_map/psum | solution.py:9
  171.9 3.8 %fusion.1 = bf16[1,8,8,8192]{3,2,0,1:T(8,128)(2,1)} fusion(bf16[64,8192]{1,0:T(8,128)(2,1)} %get-tuple-element.7, bf16[64,8192]{1,0:T(8,128)(2,1)} %get-tuple-element.8, bf16[1,8,8,8192]{3,2,0,1:T(8,128)(2,1)S(1)} %all-to-all-done), kind=kOutput, calls=%fused_computation.5 | convolution fusion | flops 134746112 | bytes 4194304 | tf_op jit(solution)/shard_map/scnr,srd->scnd/dot_general | solution.py:25
  175.7 3.8 %all-to-all-start.1 = ((bf16[1,8,8,8192]{3,2,0,1:T(8,128)(2,1)}), bf16[1,8,8,8192]{3,2,0,1:T(8,128)(2,1)S(1)}, u32[]{:S(2)}, u32[]{:S(2)}) async-start(bf16[1,8,8,8192]{3,2,0,1:T(8,128)(2,1)} %fusion.1), calls=%async_computation.1 | async-start | bytes 2097152 | tf_op jit(solution)/shard_map/all_to_all | solution.py:32
  179.5 3.5 %fusion.3 = bf16[1,8,8,8192]{3,2,0,1:T(8,128)(2,1)} fusion(bf16[64,8192]{1,0:T(8,128)(2,1)S(1)} %copy-done.1, bf16[64,8192]{1,0:T(8,128)(2,1)} %get-tuple-element.6, bf16[1,8,8,8192]{3,2,0,1:T(8,128)(2,1)S(1)} %all-to-all-done.2), kind=kOutput, calls=%fused_computation.7 | convolution fusion | flops 134746112 | bytes 4194304 | tf_op jit(solution)/shard_map/scnr,srd->scnd/dot_general | solution.py:25
  183.0 11.9 %all-to-all-done.1 = bf16[1,8,8,8192]{3,2,0,1:T(8,128)(2,1)S(1)} async-done(((bf16[1,8,8,8192]{3,2,0,1:T(8,128)(2,1)}), bf16[1,8,8,8192]{3,2,0,1:T(8,128)(2,1)S(1)}, u32[]{:S(2)}, u32[]{:S(2)}) %all-to-all-start.1) | async-done | bytes 1048608 | tf_op jit(solution)/shard_map/all_to_all | solution.py:32
  194.9 3.6 %all-to-all-start.3 = ((bf16[1,8,8,8192]{3,2,0,1:T(8,128)(2,1)}), bf16[1,8,8,8192]{3,2,0,1:T(8,128)(2,1)S(1)}, u32[]{:S(2)}, u32[]{:S(2)}) async-start(bf16[1,8,8,8192]{3,2,0,1:T(8,128)(2,1)} %fusion.3), calls=%async_computation.3 | async-start | bytes 2097152 | tf_op jit(solution)/shard_map/all_to_all | solution.py:32
  198.5 0.4 fusion.4
  198.9 15.0 %all-to-all-done.3 = bf16[1,8,8,8192]{3,2,0,1:T(8,128)(2,1)S(1)} async-done(((bf16[1,8,8,8192]{3,2,0,1:T(8,128)(2,1)}), bf16[1,8,8,8192]{3,2,0,1:T(8,128)(2,1)S(1)}, u32[]{:S(2)}, u32[]{:S(2)}) %all-to-all-start.3) | async-done | bytes 1048608 | tf_op jit(solution)/shard_map/all_to_all | solution.py:32
  213.8 0.3 fusion.5
  214.2 1.1 pad_maximum_fusion
  (9 shorter events, 0.0 us)
Async XLA Ops:
  6.5 165.3 %all-reduce.3.cloned.1.call-start = ((), (), s32[]{:S(2)}) async-start(), calls=%async_computation.4 | async-start | bytes 8388608 | tf_op jit(solution)/shard_map/psum | solution.py:9
  13.0 0.7 copy-start.2
  13.0 1.2 copy-start
  15.8 20.6 %all-to-all-start = ((bf16[1,8,8,8192]{3,2,0,1:T(8,128)(2,1)}), bf16[1,8,8,8192]{3,2,0,1:T(8,128)(2,1)S(1)}, u32[]{:S(2)}, u32[]{:S(2)}) async-start(bf16[1,8,8,8192]{3,2,0,1:T(8,128)(2,1)} %fusion), calls=%async_computation | async-start | bytes 2097152 | tf_op jit(solution)/shard_map/all_to_all | solution.py:72
  36.4 139.3 %all-to-all-start.2 = ((bf16[1,8,8,8192]{3,2,0,1:T(8,128)(2,1)}), bf16[1,8,8,8192]{3,2,0,1:T(8,128)(2,1)S(1)}, u32[]{:S(2)}, u32[]{:S(2)}) async-start(bf16[1,8,8,8192]{3,2,0,1:T(8,128)(2,1)} %fusion.2), calls=%async_computation.2 | async-start | bytes 2097152 | tf_op jit(solution)/shard_map/all_to_all | solution.py:72
  175.7 3.8 %copy-start.1 = (bf16[64,8192]{1,0:T(8,128)(2,1)S(1)}, bf16[64,8192]{1,0:T(8,128)(2,1)}, u32[]{:S(2)}) copy-start(bf16[64,8192]{1,0:T(8,128)(2,1)} %get-tuple-element.5) | copy-start | bytes 3145732
  175.7 19.2 %all-to-all-start.1 = ((bf16[1,8,8,8192]{3,2,0,1:T(8,128)(2,1)}), bf16[1,8,8,8192]{3,2,0,1:T(8,128)(2,1)S(1)}, u32[]{:S(2)}, u32[]{:S(2)}) async-start(bf16[1,8,8,8192]{3,2,0,1:T(8,128)(2,1)} %fusion.1), calls=%async_computation.1 | async-start | bytes 2097152 | tf_op jit(solution)/shard_map/all_to_all | solution.py:32
  194.9 18.9 %all-to-all-start.3 = ((bf16[1,8,8,8192]{3,2,0,1:T(8,128)(2,1)}), bf16[1,8,8,8192]{3,2,0,1:T(8,128)(2,1)S(1)}, u32[]{:S(2)}, u32[]{:S(2)}) async-start(bf16[1,8,8,8192]{3,2,0,1:T(8,128)(2,1)} %fusion.3), calls=%async_computation.3 | async-start | bytes 2097152 | tf_op jit(solution)/shard_map/all_to_all | solution.py:32
Sparse Core Ops, SparseCore 0:
  13.1 158.7 all-reduce.2
where the time goes:
time: 223 us; the launch traced here: 222 us
  waiting for transfers between devices  173 us (78%)
  starting transfers between devices  16.1 us (7%)
  between operations  14.8 us (7%)
  matrix products  11.2 us (5%)
  other arithmetic  5.16 us (2%)
    psum x1, waiting for transfers between devices, from_root(): return lax.psum(jnp.where(mine, array, jnp.zeros_like(array)), axis)  132 us
    all_to_all x2, waiting for transfers between devices, serve_one(): lax.all_to_all(result, 'adapter', split_axis=1, concat_axis=1, tiled=True)  26.9 us
    all_to_all x2, waiting for transfers between devices, body(): lax.all_to_all(outgoing[step_index:step_index + 1], 'adapter', split_axis...  13.9 us
    all_to_all x2, starting transfers between devices, body(): lax.all_to_all(outgoing[step_index:step_index + 1], 'adapter', split_axis...  8.73 us
    all_to_all x2, starting transfers between devices, serve_one(): lax.all_to_all(result, 'adapter', split_axis=1, concat_axis=1, tiled=True)  7.39 us
    dot_general x2, matrix products, project(): jnp.einsum('scnr,srd->scnd', low_rank, stack_up, preferred_element_type=j...  7.33 us
  transfers between devices with their start and end apart: 5, of which 4 were waited for; matrix products, arithmetic and copies ran while one was open for 5% of the time, Pallas kernels for 0%

commit v1 on v0

--- a/solution.py
+++ b/solution.py
@@ -6,7 +6,7 @@
 
 def from_root(array, axis, root):
     mine = lax.axis_index(axis) == root
-    return lax.psum(jnp.where(mine, array, jnp.zeros_like(array)), axis)
+    return jnp.sum(lax.all_gather(jnp.where(mine, array, jnp.zeros_like(array)), axis), axis=0)
 
 
 def slot_matrix(column_ids, columns, capacity):

time: 223 us -> 373 us (1.67)
  waiting for transfers between devices: 173 us -> 310 us
  other arithmetic: 5.16 us -> 20 us
    all_gather x0 -> x4, waiting for transfers between devices: none -> 280 us  [from_root(): lax.all_gather(jnp.where(mine, array, jnp.zeros_like(array)), axis)]
    psum x1 -> x0, waiting for transfers between devices: 132 us -> none  [from_root(): return lax.psum(jnp.where(mine, array, jnp.zeros_like(array)), axis)]
    reduce_sum x0 -> x4, other arithmetic: none -> 14.3 us  [from_root(): jnp.sum(lax.all_gather(jnp.where(mine, array, jnp.zeros_like(array)), axi...]
    all_to_all x2, waiting for transfers between devices: 26.9 us -> 15.1 us  [serve_one(): lax.all_to_all(result, 'adapter', split_axis=1, concat_axis=1, tiled=True)]
  transfers between devices with their start and end apart: 5 -> 8, of which waited for: 4 -> 6; matrix products, arithmetic and copies ran while one was open for 5% -> 7% of each run, Pallas kernels for 0% -> 0%
where the time goes in v1:
time: 373 us
  waiting for transfers between devices  310 us (83%)
  other arithmetic  20 us (5%)
  starting transfers between devices  16.2 us (4%)
  between operations  14.4 us (4%)
  matrix products  10.8 us (3%)
    all_gather x4, waiting for transfers between devices, from_root(): lax.all_gather(jnp.where(mine, array, jnp.zeros_like(array)), axis)  280 us
    all_to_all x2, waiting for transfers between devices, serve_one(): lax.all_to_all(result, 'adapter', split_axis=1, concat_axis=1, tiled=True)  15.1 us
    reduce_sum x4, other arithmetic, from_root(): jnp.sum(lax.all_gather(jnp.where(mine, array, jnp.zeros_like(array)), axi...  14.3 us
    all_to_all x2, waiting for transfers between devices, body(): lax.all_to_all(outgoing[step_index:step_index + 1], 'adapter', split_axis...  13.9 us
    all_to_all x2, starting transfers between devices, body(): lax.all_to_all(outgoing[step_index:step_index + 1], 'adapter', split_axis...  8.73 us
  transfers between devices with their start and end apart: 8, of which 6 were waited for; matrix products, arithmetic and copies ran while one was open for 7% of the time, Pallas kernels for 0%

profile of v1, /device:TPU:0, one launch (start us, length us, event | category | flops | bytes accessed | tf_op | source)
XLA Modules:
  0.0 372.8 jit_solution(16299108334217357911)
XLA Ops:
  6.5 1.4 constant_dynamic-slice_fusion.1
  9.1 2.7 broadcast_select_fusion.3
  12.0 1.5 broadcast_select_fusion.2
  13.5 0.7 all-gather.9.cloned.1.call-update
  14.2 0.5 all-gather.11.cloned.1.call-update
  15.2 1.5 fusion
  16.8 5.2 %all-to-all-start = ((bf16[1,8,8,8192]{3,2,0,1:T(8,128)(2,1)}), bf16[1,8,8,8192]{3,2,0,1:T(8,128)(2,1)S(1)}, u32[]{:S(2)}, u32[]{:S(2)}) async-start(bf16[1,8,8,8192]{3,2,0,1:T(8,128)(2,1)} %fusion), calls=%async_computation | async-start | bytes 2097152 | tf_op jit(solution)/shard_map/all_to_all | solution.py:72
  21.9 1.5 fusion.2
  23.5 13.9 %all-to-all-done = bf16[1,8,8,8192]{3,2,0,1:T(8,128)(2,1)S(1)} async-done(((bf16[1,8,8,8192]{3,2,0,1:T(8,128)(2,1)}), bf16[1,8,8,8192]{3,2,0,1:T(8,128)(2,1)S(1)}, u32[]{:S(2)}, u32[]{:S(2)}) %all-to-all-start) | async-done | bytes 1048608 | tf_op jit(solution)/shard_map/all_to_all | solution.py:72
  37.4 3.6 all-to-all-start.2
  40.9 54.6 %all-gather.5.cloned.1.call-done = bf16[4,64,8192]{2,1,0:T(8,128)(2,1)} async-done(((bf16[1,64,8192]{2,1,0:T(8,128)(2,1)}), bf16[4,64,8192]{2,1,0:T(8,128)(2,1)}) %all-gather.5.cloned.1.call-update) | async-done | bytes 4194320 | tf_op jit(solution)/shard_map/all_gather | solution.py:9
  95.5 3.0 reduce_sum.67
  98.5 77.9 %all-gather.7.cloned.1.call-done = bf16[4,64,8192]{2,1,0:T(8,128)(2,1)} async-done(((bf16[1,64,8192]{2,1,0:T(8,128)(2,1)}), bf16[4,64,8192]{2,1,0:T(8,128)(2,1)}) %all-gather.7.cloned.1.call-update) | async-done | bytes 4194320 | tf_op jit(solution)/shard_map/all_gather | solution.py:9
  176.4 4.2 %reduce_sum.68 = bf16[64,8192]{1,0:T(8,128)(2,1)} reduce(bf16[4,64,8192]{2,1,0:T(8,128)(2,1)} %all-gather.7.cloned.1.call-done, bf16[]{:T(256)} %constant.30.clone.1), dimensions={0}, to_apply=%region_3.4 | reduce | flops 1572864 | bytes 5242882 | tf_op jit(solution)/shard_map/reduce_sum | solution.py:9
  180.6 3.6 fusion.1
  184.1 3.7 all-to-all-start.1
  187.8 69.5 %all-gather.9.cloned.1.call-done = bf16[4,64,8192]{2,1,0:T(8,128)(2,1)} async-done(((bf16[1,64,8192]{2,1,0:T(8,128)(2,1)}), bf16[4,64,8192]{2,1,0:T(8,128)(2,1)}) %all-gather.9.cloned.1.call-update) | async-done | bytes 4194320 | tf_op jit(solution)/shard_map/all_gather | solution.py:9
  257.3 3.0 reduce_sum.70
  260.3 77.7 %all-gather.11.cloned.1.call-done = bf16[4,64,8192]{2,1,0:T(8,128)(2,1)} async-done(((bf16[1,64,8192]{2,1,0:T(8,128)(2,1)}), bf16[4,64,8192]{2,1,0:T(8,128)(2,1)}) %all-gather.11.cloned.1.call-update) | async-done | bytes 4194320 | tf_op jit(solution)/shard_map/all_gather | solution.py:9
  338.1 4.2 %reduce_sum.71 = bf16[64,8192]{1,0:T(8,128)(2,1)} reduce(bf16[4,64,8192]{2,1,0:T(8,128)(2,1)} %all-gather.11.cloned.1.call-done, bf16[]{:T(256)} %constant.30.clone.1), dimensions={0}, to_apply=%region_7.8 | reduce | flops 1572864 | bytes 5242882 | tf_op jit(solution)/shard_map/reduce_sum | solution.py:9
  342.2 3.5 fusion.3
  345.7 3.7 all-to-all-start.3
  349.8 15.1 %all-to-all-done.3 = bf16[1,8,8,8192]{3,2,0,1:T(8,128)(2,1)S(1)} async-done(((bf16[1,8,8,8192]{3,2,0,1:T(8,128)(2,1)}), bf16[1,8,8,8192]{3,2,0,1:T(8,128)(2,1)S(1)}, u32[]{:S(2)}, u32[]{:S(2)}) %all-to-all-start.3) | async-done | bytes 1048608 | tf_op jit(solution)/shard_map/all_to_all | solution.py:32
  365.2 1.1 pad_maximum_fusion
  (23 shorter events, 1.3 us)
Async XLA Ops:
  6.5 5.4 %copy-start = (bf16[1,64,8192]{2,1,0:T(8,128)(2,1)S(1)}, bf16[1,64,8192]{2,1,0:T(8,128)(2,1)}, u32[]{:S(2)}) copy-start(bf16[1,64,8192]{2,1,0:T(8,128)(2,1)} %param.8) | copy-start | bytes 3145732
  6.5 89.0 %all-gather.5.cloned.1.call-start = ((), (), s32[]{:S(2)}) async-start(), calls=%async_computation.4 | async-start | bytes 5242880 | tf_op jit(solution)/shard_map/all_gather | solution.py:9
  11.9 2.9 copy-start.2
  11.9 3.4 copy-start.1
  11.9 164.5 %all-gather.7.cloned.1.call-start = ((), (), s32[]{:S(2)}) async-start(), calls=%async_computation.5 | async-start | bytes 5242880 | tf_op jit(solution)/shard_map/all_gather | solution.py:9
  13.4 243.9 %all-gather.9.cloned.1.call-start = ((), (), s32[]{:S(2)}) async-start(), calls=%async_computation.6 | async-start | bytes 5242880 | tf_op jit(solution)/shard_map/all_gather | solution.py:9
  14.2 323.9 %all-gather.11.cloned.1.call-start = ((), (), s32[]{:S(2)}) async-start(), calls=%async_computation.7 | async-start | bytes 5242880 | tf_op jit(solution)/shard_map/all_gather | solution.py:9
  16.8 20.6 %all-to-all-start = ((bf16[1,8,8,8192]{3,2,0,1:T(8,128)(2,1)}), bf16[1,8,8,8192]{3,2,0,1:T(8,128)(2,1)S(1)}, u32[]{:S(2)}, u32[]{:S(2)}) async-start(bf16[1,8,8,8192]{3,2,0,1:T(8,128)(2,1)} %fusion), calls=%async_computation | async-start | bytes 2097152 | tf_op jit(solution)/shard_map/all_to_all | solution.py:72
  37.4 146.8 %all-to-all-start.2 = ((bf16[1,8,8,8192]{3,2,0,1:T(8,128)(2,1)}), bf16[1,8,8,8192]{3,2,0,1:T(8,128)(2,1)S(1)}, u32[]{:S(2)}, u32[]{:S(2)}) async-start(bf16[1,8,8,8192]{3,2,0,1:T(8,128)(2,1)} %fusion.2), calls=%async_computation.2 | async-start | bytes 2097152 | tf_op jit(solution)/shard_map/all_to_all | solution.py:72
  184.1 161.6 %all-to-all-start.1 = ((bf16[1,8,8,8192]{3,2,0,1:T(8,128)(2,1)}), bf16[1,8,8,8192]{3,2,0,1:T(8,128)(2,1)S(1)}, u32[]{:S(2)}, u32[]{:S(2)}) async-start(bf16[1,8,8,8192]{3,2,0,1:T(8,128)(2,1)} %fusion.1), calls=%async_computation.1 | async-start | bytes 2097152 | tf_op jit(solution)/shard_map/all_to_all | solution.py:32
  345.7 19.1 %all-to-all-start.3 = ((bf16[1,8,8,8192]{3,2,0,1:T(8,128)(2,1)}), bf16[1,8,8,8192]{3,2,0,1:T(8,128)(2,1)S(1)}, u32[]{:S(2)}, u32[]{:S(2)}) async-start(bf16[1,8,8,8192]{3,2,0,1:T(8,128)(2,1)} %fusion.3), calls=%async_computation.3 | async-start | bytes 2097152 | tf_op jit(solution)/shard_map/all_to_all | solution.py:32
Sparse Core Ops, SparseCore 0:
  12.0 83.4 all-gather.4
  97.1 79.2 all-gather.6
  178.0 79.2 all-gather.8
  258.7 79.2 all-gather.10
